TPU v7x, 256 devices: a whole 4x4x8 slice. The times are simulated.
256 devices in a mesh: tm: 16 (over z_lo, x, core), space: 16 (over z_hi, y).
Axes of the slice: x: 4, y: 4, z: 8 (z_hi: 4, z_lo: 2; z = z_hi * 2 + z_lo), core: 2. Of those that a mesh axis runs over, the one named last changes fastest.
Arguments:
- tokens: bfloat16 [1680, 64, 256], P('space', 'tm'), may hold values from -11 to 11
- w_query: bfloat16 [256, 256], replicated, may hold values from -0.375 to 0.375
- w_key: bfloat16 [256, 256], replicated, may hold values from -0.375 to 0.375
- w_value: bfloat16 [256, 256], replicated, may hold values from -0.375 to 0.375
- w_out: bfloat16 [256, 256], replicated, may hold values from -0.375 to 0.375
- mask: int32 [1680, 1680], P('space'), may hold values from 0 to 1, as said below
- decay: float32 [64, 256], P('tm'), may hold values from 0 to 1
- cotangent: float32 [1680, 64, 256], P('space', 'tm'), may hold values from -6 to 6
Outputs:
- grad_tokens: float32 [1680, 64, 256], P('space', 'tm')
- grad_wq: float32 [256, 256], replicated
- grad_wk: float32 [256, 256], replicated
- grad_wv: float32 [256, 256], replicated
- output_weight_gradient: float32 [256, 256], replicated
Inputs may be any that keep to these rules, and one draw needn't show every extreme that they name: `mask`: every token may attend to itself.
All inputs are finite; a program needn't handle non-finite values.
Results may differ from a plain program's by a relative error of at most 0.03.
The roundings to bfloat16 on the way count: a program that leaves them out, or rounds other values in their place, can miss the bound.
Values may be sent and summed in bfloat16 or wider, within the bound.
A program may use at most 128 MiB of HBM per device.

v0:
```python
import math
import jax
import jax.numpy as jnp
from jax import lax
from jax.sharding import PartitionSpec as P

HEADS = 8


def shifted(array, axis, by):
    devices = lax.axis_size(axis)
    pairs = [(i, i + by) for i in range(devices) if 0 <= i + by < devices]
    return lax.ppermute(array, axis, pairs)


def project(rows_flat, weight):
    return jnp.dot(rows_flat, weight, preferred_element_type=jnp.float32).astype(jnp.bfloat16)


def cross(left, right):
    return lax.dot_general(
        left, right, (((0,), (0,)), ((), ())), preferred_element_type=jnp.float32
    )


def back_project(grads_b, weight):
    return lax.dot_general(
        grads_b, weight, (((1,), (1,)), ((), ())), preferred_element_type=jnp.float32
    )


def shards(tokens, w_query, w_key, w_value, w_out, mask, decay, cotangent):
    tok_rows, round_rows, features = tokens.shape
    head_size = features // HEADS
    score_scale = 1.0 / math.sqrt(head_size)
    x_rounds = jnp.swapaxes(tokens, 0, 1)
    flat_rows = x_rounds.reshape(-1, features)
    queries = project(flat_rows, w_query).reshape(round_rows, tok_rows, HEADS, head_size)
    own_keys = project(flat_rows, w_key).reshape(round_rows, tok_rows, features)
    own_values = project(flat_rows, w_value).reshape(round_rows, tok_rows, features)
    all_keys, all_values = (
        lax.all_gather(own_keys, "space", axis=1, tiled=True),
        lax.all_gather(own_values, "space", axis=1, tiled=True),
    )
    random_key_count = all_keys.shape[1]
    all_keys = all_keys.reshape(round_rows, random_key_count, HEADS, head_size)
    all_values = all_values.reshape(round_rows, random_key_count, HEADS, head_size)
    allowed = mask > 0

    def masked_scores(q_round, k_round):
        scores = (
            jnp.einsum("ihe,jhe->hij", q_round, k_round, preferred_element_type=jnp.float32)
            * score_scale
        )
        return jnp.where(allowed[None], scores, -1e30)

    def forward(round_index):
        scores = masked_scores(queries[round_index], all_keys[round_index])
        maxima = jnp.max(scores, axis=2, keepdims=True)
        expons = jnp.exp(scores - maxima)
        totals = jnp.sum(expons, axis=2, keepdims=True)
        probs_b = (expons / totals).astype(jnp.bfloat16)
        stack_result_matrix = jnp.einsum(
            "hij,jhe->ihe", probs_b, all_values[round_index], preferred_element_type=jnp.float32
        )
        return (stack_result_matrix.astype(jnp.bfloat16), maxima, totals)

    attended, maxima, totals = lax.map(forward, jnp.arange(round_rows))
    local_grads = [None] * round_rows
    reach = [None] * round_rows
    local_grads[round_rows - 1] = cotangent[:, round_rows - 1]
    reach[round_rows - 1] = jnp.ones((1, features), jnp.float32)
    for position in range(round_rows - 2, -1, -1):
        local_grads[position] = (
            cotangent[:, position] + decay[position + 1][None] * local_grads[position + 1]
        )
        reach[position] = decay[position + 1][None] * reach[position + 1]
    block_decay = decay[0][None] * reach[0]
    block_update_message = decay[0][None] * local_grads[0]

    def relay(step_index, state):
        incoming, message = state
        incoming = shifted(message.astype(jnp.bfloat16), "tm", -1).astype(message.dtype)
        return (incoming, block_update_message + block_decay * incoming)

    carried, unused = lax.fori_loop(
        0, lax.axis_size("tm"), relay, (jnp.zeros_like(block_update_message), block_update_message)
    )
    grads = jnp.stack(
        [local_grads[position] + reach[position] * carried for position in range(round_rows)],
        axis=0,
    )
    grads_flat = grads.astype(jnp.bfloat16).reshape(-1, features)
    attended_flat = attended.reshape(-1, features)
    output_weight_gradient = cross(attended_flat, grads_flat)
    upstream = (
        back_project(grads_flat, w_out)
        .astype(jnp.bfloat16)
        .reshape(round_rows, tok_rows, HEADS, head_size)
    )
    deltas = jnp.sum(upstream.astype(jnp.float32) * attended.astype(jnp.float32), axis=3)
    deltas = jnp.swapaxes(deltas, 1, 2)[..., None]

    def backward_round(round_index):
        k_round = all_keys[round_index]
        v_round = all_values[round_index]
        q_round = queries[round_index]
        up_round = upstream[round_index]
        scores = masked_scores(q_round, k_round)
        probs = jnp.exp(scores - maxima[round_index]) / totals[round_index]
        slopes = jnp.einsum("ihe,jhe->hij", up_round, v_round, preferred_element_type=jnp.float32)
        score_grads = (probs * (slopes - deltas[round_index])).astype(jnp.bfloat16)
        grad_query = (
            jnp.einsum("hij,jhe->ihe", score_grads, k_round, preferred_element_type=jnp.float32)
            * score_scale
        )
        grad_key = (
            jnp.einsum("hij,ihe->jhe", score_grads, q_round, preferred_element_type=jnp.float32)
            * score_scale
        )
        grad_value = jnp.einsum(
            "hij,ihe->jhe", probs.astype(jnp.bfloat16), up_round, preferred_element_type=jnp.float32
        )
        partials = jnp.concatenate(
            [
                grad_key.reshape(random_key_count, features),
                grad_value.reshape(random_key_count, features),
            ],
            axis=1,
        )
        partials = partials.astype(jnp.bfloat16).astype(jnp.float32)
        return (grad_query.astype(jnp.bfloat16), partials)

    grad_queries, partial_terms = lax.map(backward_round, jnp.arange(round_rows))
    partial_terms = jnp.swapaxes(partial_terms, 0, 1)
    kv_grads = lax.psum_scatter(
        partial_terms.astype(jnp.bfloat16), "space", scatter_dimension=0, tiled=True
    ).astype(jnp.float32)
    kv_grads = jnp.swapaxes(kv_grads, 0, 1)
    grad_keys = kv_grads[..., :features].astype(jnp.bfloat16).reshape(-1, features)
    grad_values = kv_grads[..., features:].astype(jnp.bfloat16).reshape(-1, features)
    grad_q_flat = grad_queries.reshape(-1, features)
    grad_rows = grads.reshape(-1, features) + back_project(grad_q_flat, w_query)
    grad_rows = grad_rows + back_project(grad_keys, w_key) + back_project(grad_values, w_value)
    grad_tokens = jnp.swapaxes(grad_rows.reshape(round_rows, tok_rows, features), 0, 1)
    summed = lax.psum(
        (
            cross(flat_rows, grad_q_flat),
            cross(flat_rows, grad_keys),
            cross(flat_rows, grad_values),
            output_weight_gradient,
        ),
        ("tm", "space"),
    )
    return (grad_tokens, summed[0], summed[1], summed[2], summed[3])


def solution(mesh):
    return jax.shard_map(
        shards,
        mesh=mesh,
        in_specs=(
            P("space", "tm", None),
            P(),
            P(),
            P(),
            P(),
            P("space", None),
            P("tm", None),
            P("space", "tm", None),
        ),
        out_specs=(P("space", "tm", None), P(), P(), P(), P()),
        check_vma=False,
    )
```

profile of v0, /device:TPU:8, one launch (start us, length us, event | category | flops | bytes accessed | tf_op | source)
XLA Modules:
  0.0 1136.6 jit_solution(881701952524546462)
XLA Ops:
  14.5 117.5 %while.38 = (s32[]{:T(128)}, f32[105,256]{1,0:T(8,128)}, bf16[105,256]{1,0:T(8,128)(2,1)S(1)}, f32[1,256]{1,0:T(1,128)S(1)}, f32[105,256]{1,0:T(8,128)S(1)}, /*index=5*/s32[]{:T(128)}) while((s32[]{:T(128)}, f32[105,256]{1,0:T(8,128)}, bf16[105,256]{1,0:T(8,128)(2,1)S(1)}, f32[1,256]{1,0:T(1,128)S(1)}, f32[105,256]{1,0:T(8,128)S(1)}, ...), condition=%wide.region_1.2_spmd, body=%wide.region_0.1_spmd.sunk | while | flops 107522 | bytes 538733 | solution.py:86
  19.6 3.6 collective-permute-done
  25.1 4.2 collective-permute-done
  31.3 4.6 collective-permute-done
  37.8 4.6 collective-permute-done
  44.4 4.2 collective-permute-done
  50.5 4.2 collective-permute-done
  56.7 4.6 collective-permute-done
  63.2 4.6 collective-permute-done
  69.8 4.6 collective-permute-done
  76.3 5.4 collective-permute-done
  83.7 10.1 collective-permute-done
  95.7 10.1 collective-permute-done
  107.8 7.1 collective-permute-done
  116.8 6.3 collective-permute-done
  125.1 6.3 collective-permute-done
  134.7 6.9 copy.82
  141.5 12.3 %all-gather.5.cloned.1.call-done = bf16[4,1680,256]{2,0,1:T(4,128)(2,1)} async-done(((bf16[4,105,256]{2,0,1:T(4,128)(2,1)}), bf16[4,1680,256]{2,0,1:T(4,128)(2,1)}) %all-gather.5.cloned.1.call-update) | async-done | bytes 3440656 | tf_op jit(solution)/shard_map/all_gather | solution.py:43
  153.8 6.9 copy.85
  160.8 39.1 %while.39 = (s32[]{:T(128)}, bf16[4,105,8,32]{1,3,2,0:T(8,128)(2,1)S(1)}, f32[4,8,105,1]{2,1,3,0:T(8,128)S(1)}, f32[4,8,105,1]{2,1,3,0:T(8,128)S(1)}, s32[4]{0:T...) while((s32[]{:T(128)}, ...), condition=%wide.region_5.6_spmd, body=%wide.region_2.5_spmd.sunk | while | flops 197593216 | bytes 20291880 | solution.py:68
  200.2 316.6 %while.40 = (s32[]{:T(128)}, bf16[4,105,8,32]{1,3,2,0:T(8,128)(2,1)S(1)}, bf16[4,1680,512]{2,0,1:T(4,128)(2,1)}, s32[4]{0:T(128)S(1)}, bf16[4,1680,8,32]{1,3,2,0...) while((s32[]{:T(128)}, ...), condition=%wide.region_8.9_spmd, body=%wide.region_7.8_spmd.sunk | while | flops 467658240 | bytes 43092636 | solution.py:134
  212.0 6.3 copy.148
  218.4 61.0 %dynamic_update_slice.29 = bf16[4,1680,512]{2,0,1:T(4,128)(2,1)} dynamic-update-slice(bf16[4,1680,512]{2,0,1:T(4,128)(2,1)} %get-tuple-element.583, bf16[1,1680,512]{2,0,1:T(2,128)(2,1)} %copy.148, s32[]{:T(128)S(6)} %copy.178, s32[]{:T(128)} %constant.35.clone.1..sunk.1, s32[]{:T(128)} %constant.35.clone.1..sunk.1) | dynamic-update-slice | bytes 3440644 | tf_op jit(solution)/shard_map/while/body/jit(dynamic_update_index_in_dim)/dynamic_update_slice | solution.py:134
  281.9 3.4 exponential_divide_fusion.2
  291.2 6.3 copy.148
  297.5 61.0 %dynamic_update_slice.29 = bf16[4,1680,512]{2,0,1:T(4,128)(2,1)} dynamic-update-slice(bf16[4,1680,512]{2,0,1:T(4,128)(2,1)} %get-tuple-element.583, bf16[1,1680,512]{2,0,1:T(2,128)(2,1)} %copy.148, s32[]{:T(128)S(6)} %copy.178, s32[]{:T(128)} %constant.35.clone.1..sunk.1, s32[]{:T(128)} %constant.35.clone.1..sunk.1) | dynamic-update-slice | bytes 3440644 | tf_op jit(solution)/shard_map/while/body/jit(dynamic_update_index_in_dim)/dynamic_update_slice | solution.py:134
  370.3 6.3 copy.148
  376.7 61.0 %dynamic_update_slice.29 = bf16[4,1680,512]{2,0,1:T(4,128)(2,1)} dynamic-update-slice(bf16[4,1680,512]{2,0,1:T(4,128)(2,1)} %get-tuple-element.583, bf16[1,1680,512]{2,0,1:T(2,128)(2,1)} %copy.148, s32[]{:T(128)S(6)} %copy.178, s32[]{:T(128)} %constant.35.clone.1..sunk.1, s32[]{:T(128)} %constant.35.clone.1..sunk.1) | dynamic-update-slice | bytes 3440644 | tf_op jit(solution)/shard_map/while/body/jit(dynamic_update_index_in_dim)/dynamic_update_slice | solution.py:134
  449.5 6.3 copy.148
  455.8 61.0 %dynamic_update_slice.29 = bf16[4,1680,512]{2,0,1:T(4,128)(2,1)} dynamic-update-slice(bf16[4,1680,512]{2,0,1:T(4,128)(2,1)} %get-tuple-element.583, bf16[1,1680,512]{2,0,1:T(2,128)(2,1)} %copy.148, s32[]{:T(128)S(6)} %copy.178, s32[]{:T(128)} %constant.35.clone.1..sunk.1, s32[]{:T(128)} %constant.35.clone.1..sunk.1) | dynamic-update-slice | bytes 3440644 | tf_op jit(solution)/shard_map/while/body/jit(dynamic_update_index_in_dim)/dynamic_update_slice | solution.py:134
  522.2 331.0 %all-reduce.5.cloned.1.call-done = bf16[1680,4,512]{2,1,0:T(4,128)(2,1)} async-done(((bf16[1680,4,512]{2,1,0:T(4,128)(2,1)}), bf16[1680,4,512]{2,1,0:T(4,128)(2,1)}) %all-reduce.5.cloned.1.call-update) | async-done | bytes 6881296
  858.3 264.8 %all-reduce.7.cloned.1.call-done = (f32[256,256]{0,1:T(8,128)}, f32[256,256]{0,1:T(8,128)}, f32[256,256]{0,1:T(8,128)}, f32[256,256]{1,0:T(8,128)}) async-done(((f32[256,256]{0,1:T(8,128)}, f32[256,256]{0,1:T(8,128)}, f32[256,256]{0,1:T(8,128)}, f32[256,256]{1,0:T(8,128)}), (f32[256,256]{0,1:T(8,128)}, f32[256,256]{0,1:T(8,128)}, f32[256,256]{0,1:T(8,128)}, ...) | async-done | bytes 1048592 | tf_op jit(solution)/shard_map/psum | solution.py:146
  (194 shorter events, 126.7 us)
Async XLA Ops:
  7.2 5.5 copy-start
  7.2 7.0 copy-start.16
  7.2 126.6 %copy-start.18 = (bf16[256,256]{1,0:T(8,128)(2,1)S(1)}, bf16[256,256]{1,0:T(8,128)(2,1)}, u32[]{:S(2)}) copy-start(bf16[256,256]{1,0:T(8,128)(2,1)} %param.18) | copy-start | bytes 393220
  7.2 127.5 %all-gather.3.cloned.1.call-start = ((), (), s32[]{:S(2)}) async-start(), calls=%async_computation | async-start | bytes 3655680 | tf_op jit(solution)/shard_map/all_gather | solution.py:42
  8.3 125.9 %copy-start.1 = (bf16[420,256]{1,0:T(8,128)(2,1)}, bf16[420,256]{1,0:T(8,128)(2,1)S(1)}, u32[]{:S(2)}) copy-start(bf16[420,256]{1,0:T(8,128)(2,1)S(1)} %reshape.106) | copy-start | bytes 645124
  10.4 124.1 %copy-start.13 = (s32[105,1680]{1,0:T(8,128)S(1)}, s32[105,1680]{1,0:T(8,128)}, u32[]{:S(2)}) copy-start(s32[105,1680]{1,0:T(8,128)} %param.19) | copy-start | bytes 2116804
  10.5 143.4 %all-gather.5.cloned.1.call-start = ((), (), s32[]{:S(2)}) async-start(), calls=%async_computation.1 | async-start | bytes 3655680 | tf_op jit(solution)/shard_map/all_gather | solution.py:43
  12.6 840.6 %all-reduce.5.cloned.1.call-start = ((), (), s32[]{:S(2)}) async-start(), calls=%async_computation.2 | async-start | bytes 13762560
  14.5 3.1 collective-permute-start
  18.3 4.9 collective-permute-start
  23.9 5.5 collective-permute-start
  30.0 5.9 collective-permute-start
  36.5 5.9 collective-permute-start
  43.1 5.5 collective-permute-start
  49.2 5.5 collective-permute-start
  55.4 5.9 collective-permute-start
  61.9 5.9 collective-permute-start
  68.5 5.9 collective-permute-start
  75.0 6.7 collective-permute-start
  82.4 11.3 collective-permute-start
  94.4 11.4 %collective-permute-start = (bf16[105,256]{1,0:T(8,128)(2,1)S(1)}, bf16[105,256]{1,0:T(8,128)(2,1)S(1)}, u32[]{:S(2)}, u32[]{:S(2)}) collective-permute-start(bf16[105,256]{1,0:T(8,128)(2,1)S(1)} %get-tuple-element.520), channel_id=1, source_target_pairs={{16,0},{32,16},{48,32},{64,48},{80,64},{96,80},{112,96},{128,112},... | collective-permute-start | bytes 161288 | tf_op jit(solution)/shard_map/while/body/eval_jaxpr/ppermute | solution.py:13
  106.5 8.4 collective-permute-start
  115.5 7.6 collective-permute-start
  123.8 7.6 collective-permute-start
  133.0 1.4 copy-start.5
  133.8 26.9 %copy-start.3 = (f32[420,256]{1,0:T(8,128)}, f32[420,256]{1,0:T(8,128)S(1)}, u32[]{:S(2)}) copy-start(f32[420,256]{1,0:T(8,128)S(1)} %reshape.105) | copy-start | bytes 1290244
  516.8 3.2 copy-start.2
  516.8 5.1 copy-start.4
  516.8 337.7 %copy-start.17 = (bf16[105,4,256]{2,1,0:T(4,128)(2,1)S(1)}, bf16[105,4,256]{2,1,0:T(4,128)(2,1)}, u32[]{:S(2)}) copy-start(bf16[105,4,256]{2,1,0:T(4,128)(2,1)} %param.14) | copy-start | bytes 645124
  516.9 339.8 %copy-start.14 = (bf16[256,256]{1,0:T(8,128)(2,1)S(1)}, bf16[256,256]{1,0:T(8,128)(2,1)}, u32[]{:S(2)}) copy-start(bf16[256,256]{1,0:T(8,128)(2,1)} %param.16) | copy-start | bytes 393220
  516.9 606.2 %all-reduce.7.cloned.1.call-start = ((), (), s32[]{:S(2)}) async-start(), calls=%async_computation.3 | async-start | bytes 2097152 | tf_op jit(solution)/shard_map/psum | solution.py:146
  517.9 339.0 %copy-start.15 = (bf16[256,256]{1,0:T(8,128)(2,1)S(1)}, bf16[256,256]{1,0:T(8,128)(2,1)}, u32[]{:S(2)}) copy-start(bf16[256,256]{1,0:T(8,128)(2,1)} %param.17) | copy-start | bytes 393220
  (8 other events, 7.1 us)
Sparse Core Ops, SparseCore 0:
  11.0 71.6 all-gather.2
  85.7 68.0 all-gather.4
  517.0 336.1 all-reduce.4
  860.4 262.5 all-reduce.6
where the time goes:
time: 1160 us; the launch traced here: 1140 us
  waiting for transfers between devices  694 us (60%)
  local copies, waits for them, and re-layouts  304 us (26%)
  matrix products  66.1 us (6%)
  starting transfers between devices  20.8 us (2%)
  other arithmetic  20 us (2%)
  loops' own time  16.1 us (1%)
  between operations  15 us (1%)
    unnamed x5, waiting for transfers between devices  331 us
    dynamic_update_slice x8, local copies, waits for them, and re-layouts, shards(): lax.map(backward_round, jnp.arange(round_rows))  269 us
    psum x1, waiting for transfers between devices, shards(): lax.psum((cross(flat_rows, grad_q_flat), cross(flat_rows, grad_keys), cro...  265 us
    ppermute x16, waiting for transfers between devices, shifted(): return lax.ppermute(array, axis, pairs)  86.3 us
    dot_general x8, matrix products, masked_scores(): jnp.einsum('ihe,jhe->hij', q_round, k_round, preferred_element_type=jnp.f...  23.9 us
  transfers between devices with their start and end apart: 20, of which 19 were waited for; matrix products, arithmetic and copies ran while one was open for 3% of the time, Pallas kernels for 0%

commit v1 on v0

--- a/solution.py
+++ b/solution.py
@@ -1,3 +1,4 @@
+import functools
 import math
 import jax
 import jax.numpy as jnp
@@ -5,6 +6,15 @@
 from jax.sharding import PartitionSpec as P
 
 HEADS = 8
+
+
+def ports_hold(field, named_axis, shard_axis):
+    for num in (named_axis, shard_axis):
+        field = lax.psum(field, num)
+    return field
+
+
+bring_inputs = functools.partial(ports_hold, named_axis="space", shard_axis="tm")
 
 
 def shifted(array, axis, by):
@@ -143,14 +153,13 @@
     grad_rows = grads.reshape(-1, features) + back_project(grad_q_flat, w_query)
     grad_rows = grad_rows + back_project(grad_keys, w_key) + back_project(grad_values, w_value)
     grad_tokens = jnp.swapaxes(grad_rows.reshape(round_rows, tok_rows, features), 0, 1)
-    summed = lax.psum(
+    summed = bring_inputs(
         (
             cross(flat_rows, grad_q_flat),
             cross(flat_rows, grad_keys),
             cross(flat_rows, grad_values),
             output_weight_gradient,
-        ),
-        ("tm", "space"),
+        )
     )
     return (grad_tokens, summed[0], summed[1], summed[2], summed[3])
 

time: 1160 us -> 1190 us (1.026)
  waiting for transfers between devices: 694 us -> 730 us
    psum x1 -> x2, waiting for transfers between devices: 265 us -> 299 us  [ports_hold(): field = lax.psum(field, num)]
    unnamed x5 -> x6, waiting for transfers between devices: 331 us -> 332 us
  transfers between devices with their start and end apart: 20 -> 21, of which waited for: 19 -> 20; matrix products, arithmetic and copies ran while one was open for 3% -> 2% of each run, Pallas kernels for 0% -> 0%
where the time goes in v1:
time: 1190 us; the launch traced here: 1170 us
  waiting for transfers between devices  730 us (61%)
  local copies, waits for them, and re-layouts  304 us (26%)
  matrix products  66.4 us (6%)
  starting transfers between devices  20.9 us (2%)
  other arithmetic  20.2 us (2%)
  loops' own time  16.1 us (1%)
  between operations  15 us (1%)
    unnamed x6, waiting for transfers between devices  332 us
    psum x2, waiting for transfers between devices, ports_hold(): field = lax.psum(field, num)  299 us
    dynamic_update_slice x8, local copies, waits for them, and re-layouts, shards(): lax.map(backward_round, jnp.arange(round_rows))  269 us
    ppermute x16, waiting for transfers between devices, shifted(): return lax.ppermute(array, axis, pairs)  86.3 us
    dot_general x8, matrix products, masked_scores(): jnp.einsum('ihe,jhe->hij', q_round, k_round, preferred_element_type=jnp.f...  23.9 us
  transfers between devices with their start and end apart: 21, of which 20 were waited for; matrix products, arithmetic and copies ran while one was open for 2% of the time, Pallas kernels for 0%

profile of v1, /device:TPU:8, one launch (start us, length us, event | category | flops | bytes accessed | tf_op | source)
XLA Modules:
  0.0 1172.0 jit_solution(16082452209460414612)
XLA Ops:
  14.5 117.6 %while.38 = (s32[]{:T(128)}, f32[105,256]{1,0:T(8,128)}, bf16[105,256]{1,0:T(8,128)(2,1)S(1)}, f32[1,256]{1,0:T(1,128)S(1)}, f32[105,256]{1,0:T(8,128)S(1)}, /*index=5*/s32[]{:T(128)}) while((s32[]{:T(128)}, f32[105,256]{1,0:T(8,128)}, bf16[105,256]{1,0:T(8,128)(2,1)S(1)}, f32[1,256]{1,0:T(1,128)S(1)}, f32[105,256]{1,0:T(8,128)S(1)}, ...), condition=%wide.region_1.2_spmd, body=%wide.region_0.1_spmd.sunk | while | flops 107522 | bytes 538733 | solution.py:96
  19.6 3.6 collective-permute-done
  25.1 4.2 collective-permute-done
  31.3 4.6 collective-permute-done
  37.8 4.6 collective-permute-done
  44.4 4.2 collective-permute-done
  50.5 4.2 collective-permute-done
  56.7 4.6 collective-permute-done
  63.2 4.6 collective-permute-done
  69.8 4.6 collective-permute-done
  76.3 5.4 collective-permute-done
  83.7 10.0 collective-permute-done
  95.7 10.1 collective-permute-done
  107.8 7.1 collective-permute-done
  116.9 6.2 collective-permute-done
  125.0 6.4 collective-permute-done
  134.7 6.9 copy.82
  141.7 12.1 %all-gather.5.cloned.1.call-done = bf16[4,1680,256]{2,0,1:T(4,128)(2,1)} async-done(((bf16[4,105,256]{2,0,1:T(4,128)(2,1)}), bf16[4,1680,256]{2,0,1:T(4,128)(2,1)}) %all-gather.5.cloned.1.call-update) | async-done | bytes 3440656 | tf_op jit(solution)/shard_map/all_gather | solution.py:53
  153.8 6.8 copy.85
  160.7 39.7 %while.39 = (s32[]{:T(128)}, bf16[4,105,8,32]{1,3,2,0:T(8,128)(2,1)S(1)}, f32[4,8,105,1]{2,1,3,0:T(8,128)S(1)}, f32[4,8,105,1]{2,1,3,0:T(8,128)S(1)}, s32[4]{0:T...) while((s32[]{:T(128)}, ...), condition=%wide.region_5.6_spmd, body=%wide.region_2.5_spmd.sunk | while | flops 197593216 | bytes 20291880 | solution.py:78
  200.7 316.2 %while.40 = (s32[]{:T(128)}, bf16[4,105,8,32]{1,3,2,0:T(8,128)(2,1)S(1)}, bf16[4,1680,512]{2,0,1:T(4,128)(2,1)}, s32[4]{0:T(128)S(1)}, bf16[4,1680,8,32]{1,3,2,0...) while((s32[]{:T(128)}, ...), condition=%wide.region_8.9_spmd, body=%wide.region_7.8_spmd.sunk | while | flops 467658240 | bytes 43092636 | solution.py:144
  212.5 6.3 copy.148
  218.8 60.9 %dynamic_update_slice.29 = bf16[4,1680,512]{2,0,1:T(4,128)(2,1)} dynamic-update-slice(bf16[4,1680,512]{2,0,1:T(4,128)(2,1)} %get-tuple-element.587, bf16[1,1680,512]{2,0,1:T(2,128)(2,1)} %copy.148, s32[]{:T(128)S(6)} %copy.178, s32[]{:T(128)} %constant.35.clone.1..sunk.1, s32[]{:T(128)} %constant.35.clone.1..sunk.1) | dynamic-update-slice | bytes 3440644 | tf_op jit(solution)/shard_map/while/body/jit(dynamic_update_index_in_dim)/dynamic_update_slice | solution.py:144
  291.6 6.3 copy.148
  297.9 60.9 %dynamic_update_slice.29 = bf16[4,1680,512]{2,0,1:T(4,128)(2,1)} dynamic-update-slice(bf16[4,1680,512]{2,0,1:T(4,128)(2,1)} %get-tuple-element.587, bf16[1,1680,512]{2,0,1:T(2,128)(2,1)} %copy.148, s32[]{:T(128)S(6)} %copy.178, s32[]{:T(128)} %constant.35.clone.1..sunk.1, s32[]{:T(128)} %constant.35.clone.1..sunk.1) | dynamic-update-slice | bytes 3440644 | tf_op jit(solution)/shard_map/while/body/jit(dynamic_update_index_in_dim)/dynamic_update_slice | solution.py:144
  370.6 6.3 copy.148
  376.9 60.9 %dynamic_update_slice.29 = bf16[4,1680,512]{2,0,1:T(4,128)(2,1)} dynamic-update-slice(bf16[4,1680,512]{2,0,1:T(4,128)(2,1)} %get-tuple-element.587, bf16[1,1680,512]{2,0,1:T(2,128)(2,1)} %copy.148, s32[]{:T(128)S(6)} %copy.178, s32[]{:T(128)} %constant.35.clone.1..sunk.1, s32[]{:T(128)} %constant.35.clone.1..sunk.1) | dynamic-update-slice | bytes 3440644 | tf_op jit(solution)/shard_map/while/body/jit(dynamic_update_index_in_dim)/dynamic_update_slice | solution.py:144
  449.7 6.3 copy.148
  456.0 60.9 %dynamic_update_slice.29 = bf16[4,1680,512]{2,0,1:T(4,128)(2,1)} dynamic-update-slice(bf16[4,1680,512]{2,0,1:T(4,128)(2,1)} %get-tuple-element.587, bf16[1,1680,512]{2,0,1:T(2,128)(2,1)} %copy.148, s32[]{:T(128)S(6)} %copy.178, s32[]{:T(128)} %constant.35.clone.1..sunk.1, s32[]{:T(128)} %constant.35.clone.1..sunk.1) | dynamic-update-slice | bytes 3440644 | tf_op jit(solution)/shard_map/while/body/jit(dynamic_update_index_in_dim)/dynamic_update_slice | solution.py:144
  522.0 332.0 %all-reduce.7.cloned.1.call-done = bf16[1680,4,512]{2,1,0:T(4,128)(2,1)} async-done(((bf16[1680,4,512]{2,1,0:T(4,128)(2,1)}), bf16[1680,4,512]{2,1,0:T(4,128)(2,1)}) %all-reduce.7.cloned.1.call-update) | async-done | bytes 6881296
  857.4 174.9 %all-reduce.9.cloned.1.call-done = (f32[256,256]{0,1:T(8,128)}, f32[256,256]{0,1:T(8,128)}, f32[256,256]{0,1:T(8,128)}, f32[256,256]{1,0:T(8,128)}) async-done(((f32[256,256]{0,1:T(8,128)}, f32[256,256]{0,1:T(8,128)}, f32[256,256]{0,1:T(8,128)}, f32[256,256]{1,0:T(8,128)}), (f32[256,256]{0,1:T(8,128)}, f32[256,256]{0,1:T(8,128)}, f32[256,256]{0,1:T(8,128)}, ...) | async-done | bytes 1048592 | tf_op jit(solution)/shard_map/psum | solution.py:13
  1034.4 124.0 %all-reduce.11.cloned.1.call-done = (f32[256,256]{0,1:T(8,128)}, f32[256,256]{0,1:T(8,128)}, f32[256,256]{0,1:T(8,128)}, f32[256,256]{1,0:T(8,128)}) async-done(((f32[256,256]{0,1:T(8,128)}, f32[256,256]{0,1:T(8,128)}, f32[256,256]{0,1:T(8,128)}, f32[256,256]{1,0:T(8,128)}), (f32[256,256]{0,1:T(8,128)}, f32[256,256]{0,1:T(8,128)}, f32[256,256]{0,1:T(8,128)}, ...) | async-done | bytes 1048592 | tf_op jit(solution)/shard_map/psum | solution.py:13
  (197 shorter events, 130.6 us)
Async XLA Ops:
  7.2 5.5 copy-start
  7.2 7.0 copy-start.16
  7.2 126.7 %copy-start.18 = (bf16[256,256]{1,0:T(8,128)(2,1)S(1)}, bf16[256,256]{1,0:T(8,128)(2,1)}, u32[]{:S(2)}) copy-start(bf16[256,256]{1,0:T(8,128)(2,1)} %param.18) | copy-start | bytes 393220
  7.2 127.5 %all-gather.3.cloned.1.call-start = ((), (), s32[]{:S(2)}) async-start(), calls=%async_computation | async-start | bytes 3655680 | tf_op jit(solution)/shard_map/all_gather | solution.py:52
  8.3 126.0 %copy-start.1 = (bf16[420,256]{1,0:T(8,128)(2,1)}, bf16[420,256]{1,0:T(8,128)(2,1)S(1)}, u32[]{:S(2)}) copy-start(bf16[420,256]{1,0:T(8,128)(2,1)S(1)} %reshape.106) | copy-start | bytes 645124
  10.4 124.2 %copy-start.13 = (s32[105,1680]{1,0:T(8,128)S(1)}, s32[105,1680]{1,0:T(8,128)}, u32[]{:S(2)}) copy-start(s32[105,1680]{1,0:T(8,128)} %param.19) | copy-start | bytes 2116804
  10.5 143.3 %all-gather.5.cloned.1.call-start = ((), (), s32[]{:S(2)}) async-start(), calls=%async_computation.1 | async-start | bytes 3655680 | tf_op jit(solution)/shard_map/all_gather | solution.py:53
  12.6 841.5 %all-reduce.7.cloned.1.call-start = ((), (), s32[]{:S(2)}) async-start(), calls=%async_computation.2 | async-start | bytes 13762560
  14.5 3.1 collective-permute-start
  18.3 4.9 collective-permute-start
  23.9 5.5 collective-permute-start
  30.0 5.9 collective-permute-start
  36.5 5.9 collective-permute-start
  43.1 5.5 collective-permute-start
  49.2 5.5 collective-permute-start
  55.4 5.9 collective-permute-start
  61.9 5.9 collective-permute-start
  68.5 5.9 collective-permute-start
  75.0 6.7 collective-permute-start
  82.4 11.3 collective-permute-start
  94.4 11.4 collective-permute-start
  106.5 8.4 collective-permute-start
  115.6 7.5 collective-permute-start
  123.8 7.7 collective-permute-start
  133.9 26.7 %copy-start.3 = (f32[420,256]{1,0:T(8,128)}, f32[420,256]{1,0:T(8,128)S(1)}, u32[]{:S(2)}) copy-start(f32[420,256]{1,0:T(8,128)S(1)} %reshape.105) | copy-start | bytes 1290244
  516.9 3.3 copy-start.2
  516.9 338.4 %copy-start.17 = (bf16[105,4,256]{2,1,0:T(4,128)(2,1)S(1)}, bf16[105,4,256]{2,1,0:T(4,128)(2,1)}, u32[]{:S(2)}) copy-start(bf16[105,4,256]{2,1,0:T(4,128)(2,1)} %param.14) | copy-start | bytes 645124
  517.0 515.3 %copy-start.4 = (f32[420,256]{1,0:T(8,128)S(1)}, f32[420,256]{1,0:T(8,128)}, u32[]{:S(2)}) copy-start(f32[420,256]{1,0:T(8,128)} %copy-done.3) | copy-start | bytes 1290244
  517.0 515.3 %all-reduce.9.cloned.1.call-start = ((), (), s32[]{:S(2)}) async-start(), calls=%async_computation.3 | async-start | bytes 2097152 | tf_op jit(solution)/shard_map/psum | solution.py:13
  518.0 514.8 %copy-start.14 = (bf16[256,256]{1,0:T(8,128)(2,1)S(1)}, bf16[256,256]{1,0:T(8,128)(2,1)}, u32[]{:S(2)}) copy-start(bf16[256,256]{1,0:T(8,128)(2,1)} %param.16) | copy-start | bytes 393220
  519.5 513.5 %copy-start.15 = (bf16[256,256]{1,0:T(8,128)(2,1)S(1)}, bf16[256,256]{1,0:T(8,128)(2,1)}, u32[]{:S(2)}) copy-start(bf16[256,256]{1,0:T(8,128)(2,1)} %param.17) | copy-start | bytes 393220
  857.3 301.1 %all-reduce.11.cloned.1.call-start = ((), (), s32[]{:S(2)}) async-start(), calls=%async_computation.4 | async-start | bytes 2097152 | tf_op jit(solution)/shard_map/psum | solution.py:13
  (9 other events, 7.9 us)
Sparse Core Ops, SparseCore 0:
  11.0 71.6 all-gather.2
  85.8 67.9 all-gather.4
  517.1 336.9 all-reduce.6
  857.6 174.6 all-reduce.8
  1035.0 123.4 all-reduce.10
